TPU v7x, 32 devices: a whole 2x2x4 slice. The times are simulated.
32 devices in a mesh: shard: 4 (over x, core), ctx: 4 (over z), tp: 2 (over y).
Axes of the slice: x: 2, y: 2, z: 4, core: 2. Of those that a mesh axis runs over, the one named last changes fastest.
Arguments:
- tokens: bfloat16 [10240, 1024], P(('shard', 'ctx')), may hold values from -6 to 6
- cotangent: bfloat16 [10240, 1024], P(('shard', 'ctx')), may hold values from -6 to 6
- seg_ids: int32 [10240], P(('shard', 'ctx')), may hold values from 0 to 51, as said below
- positions: int32 [10240], P(('shard', 'ctx')), may hold values from 0 to 1279, as said below
- parents: int32 [52], replicated, may hold values from 0 to 51, as said below
- w_qkv: bfloat16 [3, 1024, 1024], P(None, ('shard', 'ctx'), 'tp'), may hold values from -0.1875 to 0.1875
- b_qv: float32 [2, 1024], P(None, 'tp'), may hold values from -4 to 4
- w_out: bfloat16 [1024, 1024], P('tp', ('shard', 'ctx')), may hold values from -0.5 to 0.5
- b_out: float32 [1024], replicated, may hold values from -4 to 4
- w_up: bfloat16 [1024, 4096], P(('shard', 'ctx'), 'tp'), may hold values from -0.1875 to 0.1875
- b_up: float32 [4096], P('tp'), may hold values from -4 to 4
- w_down: bfloat16 [4096, 1024], P('tp', ('shard', 'ctx')), may hold values from -0.09375 to 0.09375
- b_down: float32 [1024], replicated, may hold values from -4 to 4
- ln_gain: float32 [2, 1024], replicated, may hold values from 0.5 to 1.5
- ln_bias: float32 [2, 1024], replicated, may hold values from -3 to 3
Outputs:
- result: bfloat16 [10240, 1024], P(('shard', 'ctx'))
- grad_tokens: float32 [10240, 1024], P(('shard', 'ctx'))
- grad_w_qkv: float32 [3, 1024, 1024], P(None, ('shard', 'ctx'), 'tp')
- grad_b_qv: float32 [2, 1024], P(None, 'tp')
- grad_w_out: float32 [1024, 1024], P('tp', ('shard', 'ctx'))
- grad_b_out: float32 [1024], replicated
- grad_w_up: float32 [1024, 4096], P(('shard', 'ctx'), 'tp')
- grad_b_up: float32 [4096], P('tp')
- grad_w_down: float32 [4096, 1024], P('tp', ('shard', 'ctx'))
- grad_b_down: float32 [1024], replicated
- grad_ln_gain: float32 [2, 1024], replicated
- grad_ln_bias: float32 [2, 1024], replicated
Inputs may be any that keep to these rules, and one draw needn't show every extreme that they name: `seg_ids`: each aligned run of 2560 tokens is one tree of 13 segments: a trunk of 1024 tokens first, then 4 branches and 8 leaves of 128 tokens each, each segment's tokens adjacent and after its parent's; every segment number labels exactly one segment. Positions count from 0 at the trunk's start along the path; a segment's tokens have consecutive positions following its parent's last. `parents`: A trunk is its own parent; a branch's parent is its trunk, a leaf's parent a branch of its tree, each branch parent of two leaves.
All inputs are finite; a program needn't handle non-finite values.
Results may differ from a plain program's by a relative error of at most 0.015.
Values may be sent and summed in bfloat16 or wider, within the bound.
A program may use at most 192 MiB of HBM per device.

v0:
```python
from functools import partial
import jax
import jax.numpy as jnp
from jax import lax
from jax.sharding import PartitionSpec as P

HEADS = 16
HD = 64
KEY_BLOCK = 512
EPS = 1e-05
NEG = -1e30


def norm_forward(inputs_in, gain_row, shift_row):
    centre = inputs_in - jnp.mean(inputs_in, axis=-1, keepdims=True)
    inverse = lax.rsqrt(jnp.mean(centre * centre, axis=-1, keepdims=True) + EPS)
    normed = centre * inverse
    return (normed * gain_row + shift_row, normed, inverse)


def norm_backward(grad_in, normed, inverse, gain_row):
    scaled = grad_in * gain_row
    mean_grad = jnp.mean(scaled, axis=-1, keepdims=True)
    mean_cross = jnp.mean(scaled * normed, axis=-1, keepdims=True)
    return inverse * (scaled - mean_grad - normed * mean_cross)


def ancestry(seg_vals, parents):
    first_up = jnp.take(parents, seg_vals)
    return (first_up, jnp.take(parents, first_up))


def block_scores(query_heads, key_heads, query_tags, key_tags, slopes):
    q_seg, q_first, q_second, q_pos = query_tags
    k_seg, k_pos = key_tags
    raw_scores = jnp.einsum(
        "qhd,khd->hqk", query_heads, key_heads, preferred_element_type=jnp.float32
    ) * HD ** (-0.5)
    distance = (q_pos[:, None] - k_pos[None, :]).astype(jnp.float32)
    scores = raw_scores - slopes[:, None, None] * distance[None]
    related = (
        (k_seg[None, :] == q_seg[:, None])
        | (k_seg[None, :] == q_first[:, None])
        | (k_seg[None, :] == q_second[:, None])
    )
    allowed = related & (k_pos[None, :] <= q_pos[:, None])
    return (scores, allowed[None])


def probabilities(scores, allowed, row_max, row_sum):
    shifted = jnp.where(allowed, scores - row_max[:, :, None], NEG)
    return jnp.exp(shifted) / row_sum[:, :, None]


def per_device(
    tokens,
    cotangent,
    seg_ids,
    positions,
    parents,
    w_qkv,
    b_qv,
    w_out,
    b_out,
    w_up,
    b_up,
    w_down,
    b_down,
    ln_gain,
    ln_bias,
):
    num_rows = tokens.shape[0]
    head_count = HEADS // lax.axis_size("tp")
    head_width = head_count * HD
    head_index = (lax.axis_index("tp") * head_count + jnp.arange(head_count)).astype(jnp.float32)
    slopes = 2.0 ** (-8.0 * (head_index + 1.0) / HEADS)
    scale = HD ** (-0.5)
    full_qkv, full_out = (
        lax.all_gather(w_qkv, ("shard", "ctx"), axis=1, tiled=True),
        lax.all_gather(w_out, ("shard", "ctx"), axis=1, tiled=True),
    )
    group_seg, group_pos = (
        lax.all_gather(seg_ids, "ctx", axis=0, tiled=True),
        lax.all_gather(positions, "ctx", axis=0, tiled=True),
    )
    own_first, own_second = ancestry(seg_ids, parents)
    own_tags = (seg_ids, own_first, own_second, positions)
    inputs = tokens.astype(jnp.float32)
    norm_one, normed_one, inverse_one = norm_forward(inputs, ln_gain[0], ln_bias[0])
    act_one = norm_one.astype(jnp.bfloat16)
    projected = jnp.einsum("td,cde->cte", act_one, full_qkv, preferred_element_type=jnp.float32)
    qkv_bias = jnp.stack([b_qv[0], jnp.zeros((head_width,), jnp.float32), b_qv[1]])
    qkv_low = (projected + qkv_bias[:, None, :]).astype(jnp.bfloat16)
    query_flat, key_flat, value_flat = (qkv_low[0], qkv_low[1], qkv_low[2])
    group_keys, group_values = (
        lax.all_gather(key_flat, "ctx", axis=0, tiled=True),
        lax.all_gather(value_flat, "ctx", axis=0, tiled=True),
    )
    group_rows = group_keys.shape[0]
    block_count = group_rows // KEY_BLOCK
    key_blocks = group_keys.reshape(block_count, KEY_BLOCK, head_count, HD)
    value_blocks = group_values.reshape(block_count, KEY_BLOCK, head_count, HD)
    seg_blocks = group_seg.reshape(block_count, KEY_BLOCK)
    pos_blocks = group_pos.reshape(block_count, KEY_BLOCK)
    query_heads = query_flat.reshape(num_rows, head_count, HD)

    def stats_step(carry_in, block_parts):
        row_max, row_sum = carry_in
        key_part, seg_part, pos_part = block_parts
        scores, allowed = block_scores(
            query_heads, key_part, own_tags, (seg_part, pos_part), slopes
        )
        new_max = jnp.maximum(row_max, jnp.max(jnp.where(allowed, scores, NEG), axis=-1))
        shifted = jnp.where(allowed, scores - new_max[:, :, None], NEG)
        row_sum = row_sum * jnp.exp(row_max - new_max) + jnp.sum(jnp.exp(shifted), axis=-1)
        return ((new_max, row_sum), None)

    start_stats = (
        jnp.full((head_count, num_rows), NEG, jnp.float32),
        jnp.zeros((head_count, num_rows), jnp.float32),
    )
    (row_max, row_sum), _ = lax.scan(stats_step, start_stats, (key_blocks, seg_blocks, pos_blocks))

    def output_step(out_accum, block_parts):
        key_part, value_part, seg_part, pos_part = block_parts
        scores, allowed = block_scores(
            query_heads, key_part, own_tags, (seg_part, pos_part), slopes
        )
        prob_low = probabilities(scores, allowed, row_max, row_sum).astype(jnp.bfloat16)
        return (
            out_accum
            + jnp.einsum("hqk,khd->qhd", prob_low, value_part, preferred_element_type=jnp.float32),
            None,
        )

    attended, _ = lax.scan(
        output_step,
        jnp.zeros((num_rows, head_count, HD), jnp.float32),
        (key_blocks, value_blocks, seg_blocks, pos_blocks),
    )
    attended_low = attended.reshape(num_rows, head_width).astype(jnp.bfloat16)
    branch_one = (
        lax.psum(
            jnp.dot(attended_low, full_out, preferred_element_type=jnp.float32).astype(
                jnp.bfloat16
            ),
            "tp",
        ).astype(jnp.float32)
        + b_out
    )
    middle = inputs + branch_one
    full_up, full_down = (
        lax.all_gather(w_up, ("shard", "ctx"), axis=0, tiled=True),
        lax.all_gather(w_down, ("shard", "ctx"), axis=1, tiled=True),
    )
    norm_two, normed_two, inverse_two = norm_forward(middle, ln_gain[1], ln_bias[1])
    act_two = norm_two.astype(jnp.bfloat16)
    upper_in = jnp.dot(act_two, full_up, preferred_element_type=jnp.float32) + b_up
    gelu_vals, gelu_pull = jax.vjp(partial(jax.nn.gelu, approximate=True), upper_in)
    hidden = gelu_vals.astype(jnp.bfloat16)
    branch_two = (
        lax.psum(
            jnp.dot(hidden, full_down, preferred_element_type=jnp.float32).astype(jnp.bfloat16),
            "tp",
        ).astype(jnp.float32)
        + b_down
    )
    result = (middle + branch_two).astype(jnp.bfloat16)
    grad_out = cotangent.astype(jnp.float32)
    grad_hidden = jnp.einsum("td,fd->tf", cotangent, full_down, preferred_element_type=jnp.float32)
    grad_upper = gelu_pull(grad_hidden)[0].astype(jnp.bfloat16)
    down_term = jnp.einsum("tf,td->fd", hidden, cotangent, preferred_element_type=jnp.float32)
    up_term = jnp.einsum("td,tf->df", act_two, grad_upper, preferred_element_type=jnp.float32)
    grad_w_up, grad_w_down = (
        lax.psum_scatter(up_term, ("shard", "ctx"), scatter_dimension=0, tiled=True),
        lax.psum_scatter(down_term, ("shard", "ctx"), scatter_dimension=1, tiled=True),
    )
    grad_norm_two = lax.psum(
        jnp.einsum("tf,df->td", grad_upper, full_up, preferred_element_type=jnp.float32).astype(
            jnp.bfloat16
        ),
        "tp",
    ).astype(jnp.float32)
    grad_middle = grad_out + norm_backward(grad_norm_two, normed_two, inverse_two, ln_gain[1])
    grad_branch = grad_middle.astype(jnp.bfloat16)
    out_term = jnp.einsum(
        "te,td->ed", attended_low, grad_branch, preferred_element_type=jnp.float32
    )
    grad_att = jnp.einsum(
        "td,ed->te", grad_branch, full_out, preferred_element_type=jnp.float32
    ).astype(jnp.bfloat16)
    grad_heads = grad_att.reshape(num_rows, head_count, HD)
    row_terms = jnp.einsum("qhd,qhd->hq", grad_heads.astype(jnp.float32), attended)

    def joint_step(grad_accum, block_parts):
        key_part, value_part, seg_part, pos_part = block_parts
        scores, allowed = block_scores(
            query_heads, key_part, own_tags, (seg_part, pos_part), slopes
        )
        prob_vals = probabilities(scores, allowed, row_max, row_sum)
        grad_probs = jnp.einsum(
            "qhd,khd->hqk", grad_heads, value_part, preferred_element_type=jnp.float32
        )
        grad_scores = (prob_vals * (grad_probs - row_terms[:, :, None])).astype(jnp.bfloat16)
        grad_accum = (
            grad_accum
            + jnp.einsum("hqk,khd->qhd", grad_scores, key_part, preferred_element_type=jnp.float32)
            * scale
        )
        key_part_grad = (
            jnp.einsum("hqk,qhd->khd", grad_scores, query_heads, preferred_element_type=jnp.float32)
            * scale
        )
        value_part_grad = jnp.einsum(
            "hqk,qhd->khd",
            prob_vals.astype(jnp.bfloat16),
            grad_heads,
            preferred_element_type=jnp.float32,
        )
        return (
            grad_accum,
            (
                key_part_grad.reshape(KEY_BLOCK, head_width),
                value_part_grad.reshape(KEY_BLOCK, head_width),
            ),
        )

    grad_query_sum, (key_terms, value_terms) = lax.scan(
        joint_step,
        jnp.zeros((num_rows, head_count, HD), jnp.float32),
        (key_blocks, value_blocks, seg_blocks, pos_blocks),
    )
    key_grad_sum, value_grad_sum = (
        lax.psum_scatter(
            key_terms.reshape(group_rows, head_width).astype(jnp.bfloat16),
            "ctx",
            scatter_dimension=0,
            tiled=True,
        ).astype(jnp.float32),
        lax.psum_scatter(
            value_terms.reshape(group_rows, head_width).astype(jnp.bfloat16),
            "ctx",
            scatter_dimension=0,
            tiled=True,
        ).astype(jnp.float32),
    )
    grad_query_low = grad_query_sum.reshape(num_rows, head_width).astype(jnp.bfloat16)
    grad_key_low = key_grad_sum.astype(jnp.bfloat16)
    grad_value_low = value_grad_sum.astype(jnp.bfloat16)
    grad_qkv = jnp.stack([grad_query_low, grad_key_low, grad_value_low])
    grad_norm_one = lax.psum(
        jnp.einsum("cte,cde->td", grad_qkv, full_qkv, preferred_element_type=jnp.float32).astype(
            jnp.bfloat16
        ),
        "tp",
    ).astype(jnp.float32)
    grad_tokens = grad_middle + norm_backward(grad_norm_one, normed_one, inverse_one, ln_gain[0])
    qkv_term = jnp.einsum("td,cte->cde", act_one, grad_qkv, preferred_element_type=jnp.float32)
    grad_w_qkv, grad_w_out = (
        lax.psum_scatter(qkv_term, ("shard", "ctx"), scatter_dimension=1, tiled=True),
        lax.psum_scatter(out_term, ("shard", "ctx"), scatter_dimension=1, tiled=True),
    )
    bias_qv_part = jnp.stack(
        [
            jnp.sum(grad_query_low.astype(jnp.float32), axis=0),
            jnp.sum(grad_value_low.astype(jnp.float32), axis=0),
        ]
    )
    out_bias_part = jnp.sum(grad_branch.astype(jnp.float32), axis=0)
    up_bias_part = jnp.sum(grad_upper.astype(jnp.float32), axis=0)
    down_bias_part = jnp.sum(grad_out, axis=0)
    gain_part = jnp.stack(
        [jnp.sum(grad_norm_one * normed_one, axis=0), jnp.sum(grad_norm_two * normed_two, axis=0)]
    )
    shift_part = jnp.stack([jnp.sum(grad_norm_one, axis=0), jnp.sum(grad_norm_two, axis=0)])
    grad_b_qv, grad_b_out, grad_b_up, grad_b_down, grad_gain, grad_shift = lax.psum(
        (bias_qv_part, out_bias_part, up_bias_part, down_bias_part, gain_part, shift_part),
        ("shard", "ctx"),
    )
    return (
        result,
        grad_tokens,
        grad_w_qkv,
        grad_b_qv,
        grad_w_out,
        grad_b_out,
        grad_w_up,
        grad_b_up,
        grad_w_down,
        grad_b_down,
        grad_gain,
        grad_shift,
    )


def solution(mesh):
    placed = (
        P(("shard", "ctx"), None),
        P(("shard", "ctx"), None),
        P(("shard", "ctx")),
        P(("shard", "ctx")),
        P(),
        P(None, ("shard", "ctx"), "tp"),
        P(None, "tp"),
        P("tp", ("shard", "ctx")),
        P(),
        P(("shard", "ctx"), "tp"),
        P("tp"),
        P("tp", ("shard", "ctx")),
        P(),
        P(),
        P(),
    )
    return jax.shard_map(
        per_device,
        mesh=mesh,
        in_specs=placed,
        out_specs=(
            P(("shard", "ctx"), None),
            P(("shard", "ctx"), None),
            P(None, ("shard", "ctx"), "tp"),
            P(None, "tp"),
            P("tp", ("shard", "ctx")),
            P(),
            P(("shard", "ctx"), "tp"),
            P("tp"),
            P("tp", ("shard", "ctx")),
            P(),
            P(),
            P(),
        ),
        check_vma=False,
    )
```

profile of v0, /device:TPU:0, one launch (start us, length us, event | category | flops | bytes accessed | tf_op | source)
XLA Modules:
  0.0 1227.4 jit_solution(17177384141970764091)
XLA Ops:
  11.7 46.8 %all-gather.11.cloned.1.call-done = bf16[3,1024,512]{2,1,0:T(8,128)(2,1)} async-done(((bf16[3,64,512]{2,1,0:T(8,128)(2,1)}), bf16[3,1024,512]{2,1,0:T(8,128)(2,1)}) %all-gather.11.cloned.1.call-update) | async-done | bytes 3145744 | tf_op jit(solution)/shard_map/all_gather | solution.py:79
  58.5 4.7 fusion.83
  68.2 13.2 %all-gather.2 = s32[4,1,640]{2,1,0:T(1,128)S(1)} all-gather(s32[1,1,640]{2,1,0:T(1,128)S(1)} %reshape.676), channel_id=1, replica_groups=mesh['shard'=4,'ctx'=4,'tp'=2] {'ctx'}, dimensions={0}, use_global_device_ids=true | all-gather | bytes 12800 | tf_op jit(solution)/shard_map/all_gather | solution.py:83
  81.5 13.3 %all-gather.3 = s32[4,1,640]{2,1,0:T(1,128)S(1)} all-gather(s32[1,1,640]{2,1,0:T(1,128)S(1)} %reshape.678), channel_id=1, replica_groups=mesh['shard'=4,'ctx'=4,'tp'=2] {'ctx'}, dimensions={0}, use_global_device_ids=true | all-gather | bytes 12800 | tf_op jit(solution)/shard_map/all_gather | solution.py:84
  94.9 32.4 %select_select_fusion = (s32[640]{0:T(1024)S(1)}, s32[640]{0:T(1024)S(1)}) fusion(s32[]{:T(128)} %bitcast.57, s32[]{:T(128)} %bitcast.56, s32[]{:T(128)} %bitcast.55, s32[]{:T(128)} %bitcast.54, s32[]{:T(128)} %bitcast.53, s32[]{:T(128)} %bitcast.52, s32[]{:T(128)} %bitcast.51, s32[]{:T(128)} %bitcast.50, s32[]{:T(128)} %bitcast.49, s32[]{:T(128)} %bitcast.48, ...), kind=kLoop, calls=%fused_computation.139 | loop fusion | flops 139520 | bytes 7888 | tf_op jit(solution)/shard_map/jit(_take)/select_n | solution.py:30
  127.3 7.1 reshape.547
  134.4 4.7 copy.60
  139.0 34.5 %all-gather.21.cloned.1.call-done = bf16[1,2560,512]{1,2,0:T(8,128)(2,1)} async-done(((bf16[1,640,512]{1,2,0:T(8,128)(2,1)}), bf16[1,2560,512]{1,2,0:T(8,128)(2,1)}) %all-gather.21.cloned.1.call-update) | async-done | bytes 2621456 | tf_op jit(solution)/shard_map/all_gather | solution.py:96
  173.6 7.0 reshape.550
  180.6 4.7 copy.61
  185.3 41.6 %while.39 = (s32[]{:T(128)}, f32[8,640]{1,0:T(8,128)S(1)}, f32[8,640]{1,0:T(8,128)S(1)}, s32[5,512]{1,0:T(8,128)S(1)}, s32[640]{0:T(1024)S(1)}, /*index=5*/s32[6...) while((s32[]{:T(128)}, f32[8,640]{1,0:T(8,128)S(1)}, ...), condition=%wide.region_5.7_spmd.clone, body=%wide.region_2.6_spmd.clone.sunk | while | flops 367354912 | bytes 27360004 | solution.py:122
  185.9 4.7 select_reduce_fusion.2
  194.2 4.7 select_reduce_fusion.2
  202.6 4.8 select_reduce_fusion.2
  210.9 4.8 select_reduce_fusion.2
  219.2 4.8 select_reduce_fusion.2
  226.9 40.9 %while.40 = (s32[]{:T(128)}, f32[640,8,64]{0,2,1:T(8,128)}, bf16[5,512,8,64]{1,3,2,0:T(8,128)(2,1)}, s32[5,512]{1,0:T(8,128)S(1)}, s32[640]{0:T(1024)S(1)}, /*in...) while((s32[]{:T(128)}, f32[640,8,64]{0,2,1:T(8,128)}, ...), condition=%wide.region_7.9_spmd.clone, body=%wide.region_6.8_spmd.clone.sunk | while | flops 693043264 | bytes 7672046 | solution.py:136
  227.8 7.2 fusion.154
  235.6 7.6 fusion.154
  243.8 7.6 fusion.154
  252.0 7.6 fusion.154
  260.2 7.6 fusion.154
  274.1 43.2 %all-reduce.8.cloned.1.call-done = bf16[640,1024]{1,0:T(8,128)(2,1)} async-done(((bf16[640,1024]{1,0:T(8,128)(2,1)}), bf16[640,1024]{1,0:T(8,128)(2,1)}) %all-reduce.8.cloned.1.call-update) | async-done | bytes 1310736 | tf_op jit(solution)/shard_map/psum | solution.py:143
  319.9 50.4 %all-gather.15.cloned.1.call-done = bf16[1024,2048]{1,0:T(8,128)(2,1)} async-done(((bf16[64,2048]{1,0:T(8,128)(2,1)}), bf16[1024,2048]{1,0:T(8,128)(2,1)}) %all-gather.15.cloned.1.call-update) | async-done | bytes 4194320 | tf_op jit(solution)/shard_map/all_gather | solution.py:153
  370.3 7.7 fusion.95
  378.1 43.8 %all-gather.17.cloned.1.call-done = bf16[2048,1024]{0,1:T(8,128)(2,1)} async-done(((bf16[2048,64]{0,1:T(8,128)(2,1)}), bf16[2048,1024]{0,1:T(8,128)(2,1)}) %all-gather.17.cloned.1.call-update) | async-done | bytes 4194320 | tf_op jit(solution)/shard_map/all_gather | solution.py:154
  421.9 9.6 convert_reduce_fusion
  437.1 44.3 %all-reduce.10.cloned.1.call-done = bf16[640,1024]{1,0:T(8,128)(2,1)} async-done(((bf16[640,1024]{1,0:T(8,128)(2,1)}), bf16[640,1024]{1,0:T(8,128)(2,1)}) %all-reduce.10.cloned.1.call-update) | async-done | bytes 1310736 | tf_op jit(solution)/shard_map/psum | solution.py:178
  489.5 80.2 %while.41 = (s32[]{:T(128)}, f32[640,8,64]{0,2,1:T(8,128)S(1)}, bf16[5,512,512]{1,2,0:T(8,128)(2,1)}, bf16[5,512,512]{1,2,0:T(8,128)(2,1)}, bf16[5,512,8,64]{1,3...) while((s32[]{:T(128)}, f32[640,8,64]{0,2,1:T(8,128)S(1)}, ...), condition=%wide.region_16.18_spmd.clone, body=%wide.region_15.17_spmd.clone.sunk | while | flops 1708392448 | bytes 60513056 | solution.py:228
  490.1 5.1 fusion.165
  506.1 5.1 fusion.165
  522.2 5.1 fusion.165
  538.2 5.1 fusion.165
  554.3 5.1 fusion.165
  579.3 8.7 convolution_convert_fusion.1
  588.4 37.9 %reduce-scatter.8.cloned.1.call-done = bf16[640,512]{1,0:T(8,128)(2,1)} async-done(((bf16[2560,512]{1,0:T(8,128)(2,1)}), bf16[640,512]{1,0:T(8,128)(2,1)}) %reduce-scatter.8.cloned.1.call-update) | async-done | bytes 655376 | tf_op jit(solution)/shard_map/reduce_scatter | solution.py:240
  626.4 54.0 %reduce-scatter.6.cloned.1.call-done = bf16[640,512]{1,0:T(8,128)(2,1)} async-done(((bf16[2560,512]{1,0:T(8,128)(2,1)}), bf16[640,512]{1,0:T(8,128)(2,1)}) %reduce-scatter.6.cloned.1.call-update) | async-done | bytes 655376 | tf_op jit(solution)/shard_map/reduce_scatter | solution.py:234
  680.4 5.6 bitcast_convert_fusion
  687.5 5.8 convolution_bitcast_fusion
  693.3 9.5 copy.68
  708.0 9.7 fusion.96
  719.1 7.8 fusion.94
  729.0 31.5 %all-reduce.14.cloned.1.call-done = (bf16[640,1024]{1,0:T(8,128)(2,1)}, bf16[640,1024]{1,0:T(8,128)(2,1)}) async-done(((bf16[640,1024]{1,0:T(8,128)(2,1)}, bf16[640,1024]{1,0:T(8,128)(2,1)}), (bf16[640,1024]{1,0:T(8,128)(2,1)}, bf16[640,1024]{1,0:T(8,128)(2,1)})) %all-reduce.14.cloned.1.call-update) | async-done | bytes 2621456 | tf_op jit(solution)/shard_map/psum | solution.py:162
  763.0 65.9 %all-reduce.1 = (f32[2,512]{1,0:T(2,128)}, f32[1024]{0:T(1024)}, f32[2048]{0:T(1024)}, f32[1024]{0:T(1024)}, f32[2,1024]{1,0:T(2,128)}, /*index=5*/f32[2,1024]{1,0:T(2,128)}) all-reduce(f32[2,512]{1,0:T(2,128)S(1)} %pad_maximum_fusion.6, f32[1024]{0:T(1024)S(1)} %copy-done.32, ...), channel_id=1, replica_groups=mesh['shard'=4,'ctx'=4,'tp'=2] {'shard','ctx'}, use_global_device_ids=true, to_apply=%region_25.27 | all-reduce | flops 9216 | bytes 73728 | tf_op jit(solution)/shard_map/psum | solution.py:276
  833.4 103.3 %all-reduce.12.cloned.1.call-done = f32[3,1024,512]{2,0,1:T(4,128)} async-done(((f32[3,1024,512]{2,0,1:T(4,128)}), f32[3,1024,512]{2,0,1:T(4,128)}) %all-reduce.12.cloned.1.call-update) | async-done | bytes 6291472
  938.7 63.8 %reduce-scatter.10.cloned.1.call-done = f32[512,64]{0,1:T(8,128)} async-done(((f32[512,1024]{0,1:T(8,128)}), f32[512,64]{0,1:T(8,128)}) %reduce-scatter.10.cloned.1.call-update) | async-done | bytes 131088 | tf_op jit(solution)/shard_map/reduce_scatter | solution.py:261
  1002.5 108.7 %reduce-scatter.14.cloned.1.call-done = f32[2048,64]{0,1:T(8,128)} async-done(((f32[2048,1024]{0,1:T(8,128)}), f32[2048,64]{0,1:T(8,128)}) %reduce-scatter.14.cloned.1.call-update) | async-done | bytes 524304 | tf_op jit(solution)/shard_map/reduce_scatter | solution.py:176
  1111.2 109.4 %reduce-scatter.12.cloned.1.call-done = f32[64,2048]{1,0:T(8,128)} async-done(((f32[1024,2048]{1,0:T(8,128)}), f32[64,2048]{1,0:T(8,128)}) %reduce-scatter.12.cloned.1.call-update) | async-done | bytes 524304 | tf_op jit(solution)/shard_map/reduce_scatter | solution.py:175
  (297 shorter events, 135.1 us)
Async XLA Ops:
  7.2 51.3 %copy-start = (bf16[640,1024]{1,0:T(8,128)(2,1)S(1)}, bf16[640,1024]{1,0:T(8,128)(2,1)}, u32[]{:S(2)}) copy-start(bf16[640,1024]{1,0:T(8,128)(2,1)} %param.23) | copy-start | bytes 3932164
  7.2 4.3 copy-start.40
  7.2 4.4 copy-start.36
  7.2 4.4 copy-start.37
  7.2 51.2 %all-gather.11.cloned.1.call-start = ((), (), s32[]{:S(2)}) async-start(), calls=%async_computation.5 | async-start | bytes 3342336 | tf_op jit(solution)/shard_map/all_gather | solution.py:79
  8.0 119.3 %all-gather.19.cloned.1.call-start = ((), (), s32[]{:S(2)}) async-start(), calls=%async_computation.16 | async-start | bytes 3276800 | tf_op jit(solution)/shard_map/all_gather | solution.py:97
  9.6 48.8 %copy-start.20 = (f32[640]{0:T(1024)}, f32[640]{0:T(1024)S(1)}, u32[]{:S(2)}) copy-start(f32[640]{0:T(1024)S(1)} %broadcast_multiply_fusion.5) | copy-start | bytes 7684
  11.5 51.7 %copy-start.24 = (f32[640]{0:T(1024)}, f32[640]{0:T(1024)S(1)}, u32[]{:S(2)}) copy-start(f32[640]{0:T(1024)S(1)} %add_rsqrt_fusion.1) | copy-start | bytes 7684
  11.6 51.6 %copy-start.26 = (f32[1,1024]{1,0:T(1,128)}, f32[1,1024]{1,0:T(1,128)S(1)}, u32[]{:S(2)}) copy-start(f32[1,1024]{1,0:T(1,128)S(1)} %get-tuple-element.692) | copy-start | bytes 12292
  11.6 473.8 %copy-start.30 = (f32[1,1024]{1,0:T(1,128)}, f32[1,1024]{1,0:T(1,128)S(1)}, u32[]{:S(2)}) copy-start(f32[1,1024]{1,0:T(1,128)S(1)} %get-tuple-element.693) | copy-start | bytes 12292
  11.6 51.6 %copy-start.43 = (f32[1,1024]{1,0:T(1,128)}, f32[1,1024]{1,0:T(1,128)S(1)}, u32[]{:S(2)}) copy-start(f32[1,1024]{1,0:T(1,128)S(1)} %get-tuple-element.694) | copy-start | bytes 12292
  11.6 358.7 %copy-start.41 = (f32[1,1024]{1,0:T(1,128)}, f32[1,1024]{1,0:T(1,128)S(1)}, u32[]{:S(2)}) copy-start(f32[1,1024]{1,0:T(1,128)S(1)} %get-tuple-element.695) | copy-start | bytes 12292
  63.2 2.8 copy-start.11
  63.2 4.9 copy-start.8
  63.3 4.9 copy-start.14
  64.6 108.9 %all-gather.21.cloned.1.call-start = ((), (), s32[]{:S(2)}) async-start(), calls=%async_computation.17 | async-start | bytes 3276800 | tf_op jit(solution)/shard_map/all_gather | solution.py:96
  65.4 203.9 %all-gather.13.cloned.1.call-start = ((), (), s32[]{:S(2)}) async-start(), calls=%async_computation.6 | async-start | bytes 1114112 | tf_op jit(solution)/shard_map/all_gather | solution.py:80
  65.9 251.4 %all-reduce.8.cloned.1.call-start = ((), (), s32[]{:S(2)}) async-start(), calls=%async_computation.7 | async-start | bytes 2621440 | tf_op jit(solution)/shard_map/psum | solution.py:143
  269.3 4.1 copy-start.9
  269.3 48.0 %copy-start.18 = (f32[1024]{0:T(1024)S(1)}, f32[1024]{0:T(1024)}, u32[]{:S(2)}) copy-start(f32[1024]{0:T(1024)} %param.31) | copy-start | bytes 12292
  272.7 97.6 %all-gather.15.cloned.1.call-start = ((), (), s32[]{:S(2)}) async-start(), calls=%async_computation.8 | async-start | bytes 4456448 | tf_op jit(solution)/shard_map/all_gather | solution.py:153
  273.3 148.5 %all-gather.17.cloned.1.call-start = ((), (), s32[]{:S(2)}) async-start(), calls=%async_computation.9 | async-start | bytes 4456448 | tf_op jit(solution)/shard_map/all_gather | solution.py:154
  274.1 207.3 %all-reduce.10.cloned.1.call-start = ((), (), s32[]{:S(2)}) async-start(), calls=%async_computation.10 | async-start | bytes 2621440 | tf_op jit(solution)/shard_map/psum | solution.py:178
  319.2 166.1 %copy-start.22 = (f32[640]{0:T(1024)}, f32[640]{0:T(1024)S(1)}, u32[]{:S(2)}) copy-start(f32[640]{0:T(1024)S(1)} %broadcast_multiply_fusion.4) | copy-start | bytes 7684
  319.9 165.5 %copy-start.28 = (f32[640]{0:T(1024)}, f32[640]{0:T(1024)S(1)}, u32[]{:S(2)}) copy-start(f32[640]{0:T(1024)S(1)} %add_rsqrt_fusion) | copy-start | bytes 7684
  370.3 51.5 %copy-start.47 = (f32[2048]{0:T(1024)S(1)}, f32[2048]{0:T(1024)}, u32[]{:S(2)}) copy-start(f32[2048]{0:T(1024)} %param.33) | copy-start | bytes 24580
  421.9 11.1 copy-start.45
  437.0 189.4 %reduce-scatter.8.cloned.1.call-start = ((), (), s32[]{:S(2)}) async-start(), calls=%async_computation.12 | async-start | bytes 3276800 | tf_op jit(solution)/shard_map/reduce_scatter | solution.py:240
  481.4 4.0 copy-start.4
  481.4 4.0 copy-start.7
  481.4 4.0 copy-start.12
  485.4 2.6 copy-start.6
  485.4 2.5 copy-start.15
  574.1 106.2 %reduce-scatter.6.cloned.1.call-start = ((), (), s32[]{:S(2)}) async-start(), calls=%async_computation.11 | async-start | bytes 3276800 | tf_op jit(solution)/shard_map/reduce_scatter | solution.py:234
  578.6 181.8 %all-reduce.14.cloned.1.call-start = ((), (), s32[]{:S(2)}) async-start(), calls=%async_computation.19 | async-start | bytes 5242880 | tf_op jit(solution)/shard_map/psum | solution.py:162
  680.4 5.8 copy-start.46
  686.1 250.7 %all-reduce.12.cloned.1.call-start = ((), (), s32[]{:S(2)}) async-start(), calls=%async_computation.18 | async-start | bytes 16777216
  702.8 5.2 copy-start.13
  702.8 299.7 %reduce-scatter.10.cloned.1.call-start = ((), (), s32[]{:S(2)}) async-start(), calls=%async_computation.13 | async-start | bytes 2228224 | tf_op jit(solution)/shard_map/reduce_scatter | solution.py:261
  707.9 403.2 %reduce-scatter.14.cloned.1.call-start = ((), (), s32[]{:S(2)}) async-start(), calls=%async_computation.15 | async-start | bytes 8912896 | tf_op jit(solution)/shard_map/reduce_scatter | solution.py:176
  717.8 502.8 %reduce-scatter.12.cloned.1.call-start = ((), (), s32[]{:S(2)}) async-start(), calls=%async_computation.14 | async-start | bytes 8912896 | tf_op jit(solution)/shard_map/reduce_scatter | solution.py:175
  726.8 2.0 copy-start.17
  726.9 36.1 %copy-start.35 = (f32[1024]{0:T(1024)S(1)}, f32[1024]{0:T(1024)}, u32[]{:S(2)}) copy-start(f32[1024]{0:T(1024)} %get-tuple-element.566) | copy-start | bytes 12292
  726.9 36.1 %copy-start.34 = (f32[1024]{0:T(1024)S(1)}, f32[1024]{0:T(1024)}, u32[]{:S(2)}) copy-start(f32[1024]{0:T(1024)} %get-tuple-element.573) | copy-start | bytes 12292
  726.9 36.1 %copy-start.32 = (f32[1024]{0:T(1024)S(1)}, f32[1024]{0:T(1024)}, u32[]{:S(2)}) copy-start(f32[1024]{0:T(1024)} %get-tuple-element.672) | copy-start | bytes 12292
  726.9 36.1 %copy-start.33 = (f32[1024]{0:T(1024)S(1)}, f32[1024]{0:T(1024)}, u32[]{:S(2)}) copy-start(f32[1024]{0:T(1024)} %get-tuple-element.689) | copy-start | bytes 12292
  726.9 36.1 %copy-start.38 = (f32[2048]{0:T(1024)S(1)}, f32[2048]{0:T(1024)}, u32[]{:S(2)}) copy-start(f32[2048]{0:T(1024)} %get-tuple-element.670) | copy-start | bytes 24580
  726.9 102.0 %copy-start.39 = (f32[1024]{0:T(1024)S(1)}, f32[1024]{0:T(1024)}, u32[]{:S(2)}) copy-start(f32[1024]{0:T(1024)} %param.35) | copy-start | bytes 12292
  (18 other events, 23.9 us)
Sparse Core Ops, SparseCore 0:
  10.3 48.1 all-gather.10
  64.7 53.8 all-gather.18
  120.2 53.3 all-gather.20
  175.6 36.6 all-gather.12
  272.9 44.3 all-reduce.7
  319.6 50.6 all-gather.14
  372.8 49.0 all-gather.16
  437.1 44.2 all-reduce.9
  574.2 52.0 reduce-scatter.7
  628.5 51.7 reduce-scatter.5
  686.2 74.1 all-reduce.13
  764.5 172.2 all-reduce.11
  941.0 61.4 reduce-scatter.9
  1007.5 103.5 reduce-scatter.13
  1116.2 104.3 reduce-scatter.11
where the time goes:
time: 1230 us
  waiting for transfers between devices  775 us (63%)
  matrix products  205 us (17%)
  blocking collectives  92.4 us (8%)
  other arithmetic  76.9 us (6%)
  local copies, waits for them, and re-layouts  60.1 us (5%)
  between operations  15.5 us (1%)
    reduce_scatter x1, waiting for transfers between devices, per_device(): lax.psum_scatter(up_term, ('shard', 'ctx'), scatter_dimension=0, tiled=True)  109 us
    reduce_scatter x1, waiting for transfers between devices, per_device(): lax.psum_scatter(down_term, ('shard', 'ctx'), scatter_dimension=1, tiled=...  109 us
    unnamed x16, waiting for transfers between devices  107 us
    psum x1, blocking collectives, per_device(): lax.psum((bias_qv_part, out_bias_part, up_bias_part, down_bias_part, gain...  65.9 us
    reduce_scatter x1, waiting for transfers between devices, per_device(): lax.psum_scatter(out_term, ('shard', 'ctx'), scatter_dimension=1, tiled=T...  63.8 us
    reduce_scatter x1, waiting for transfers between devices, per_device(): lax.psum_scatter(key_terms.reshape(group_rows, head_width).astype(jnp.bfl...  54 us
    all_gather x1, waiting for transfers between devices, per_device(): lax.all_gather(w_up, ('shard', 'ctx'), axis=0, tiled=True)  50.4 us
    dot_general x10, matrix products, block_scores(): jnp.einsum('qhd,khd->hqk', query_heads, key_heads, preferred_element_type...  49.1 us
  transfers between devices with their start and end apart: 15, of which 13 were waited for; matrix products, arithmetic and copies ran while one was open for 18% of the time, Pallas kernels for 0%

commit v1 on v0

--- a/solution.py
+++ b/solution.py
@@ -274,8 +274,11 @@
     )
     shift_part = jnp.stack([jnp.sum(grad_norm_one, axis=0), jnp.sum(grad_norm_two, axis=0)])
     grad_b_qv, grad_b_out, grad_b_up, grad_b_down, grad_gain, grad_shift = lax.psum(
-        (bias_qv_part, out_bias_part, up_bias_part, down_bias_part, gain_part, shift_part),
-        ("shard", "ctx"),
+        lax.psum(
+            (bias_qv_part, out_bias_part, up_bias_part, down_bias_part, gain_part, shift_part),
+            "ctx",
+        ),
+        "shard",
     )
     return (
         result,

time: 1230 us -> 1230 us (level)
  blocking collectives: 92.4 us -> 59 us
  waiting for transfers between devices: 775 us -> 807 us
    psum x1, blocking collectives: 65.9 us -> 20.4 us  [per_device(): lax.psum((bias_qv_part, out_bias_part, up_bias_part, down_bias_part, gain...]
    unnamed x16, waiting for transfers between devices: 107 us -> 138 us
where the time goes in v1:
time: 1230 us
  waiting for transfers between devices  807 us (66%)
  matrix products  205 us (17%)
  other arithmetic  76.9 us (6%)
  local copies, waits for them, and re-layouts  60.1 us (5%)
  blocking collectives  59 us (5%)
  between operations  15.5 us (1%)
    unnamed x16, waiting for transfers between devices  138 us
    reduce_scatter x1, waiting for transfers between devices, per_device(): lax.psum_scatter(up_term, ('shard', 'ctx'), scatter_dimension=0, tiled=True)  109 us
    reduce_scatter x1, waiting for transfers between devices, per_device(): lax.psum_scatter(down_term, ('shard', 'ctx'), scatter_dimension=1, tiled=...  109 us
    reduce_scatter x1, waiting for transfers between devices, per_device(): lax.psum_scatter(out_term, ('shard', 'ctx'), scatter_dimension=1, tiled=T...  63.7 us
    reduce_scatter x1, waiting for transfers between devices, per_device(): lax.psum_scatter(key_terms.reshape(group_rows, head_width).astype(jnp.bfl...  54 us
    all_gather x1, waiting for transfers between devices, per_device(): lax.all_gather(w_up, ('shard', 'ctx'), axis=0, tiled=True)  50.4 us
    dot_general x10, matrix products, block_scores(): jnp.einsum('qhd,khd->hqk', query_heads, key_heads, preferred_element_type...  49.1 us
    all_gather x1, waiting for transfers between devices, per_device(): lax.all_gather(w_qkv, ('shard', 'ctx'), axis=1, tiled=True)  46.8 us
  transfers between devices with their start and end apart: 15, of which 13 were waited for; matrix products, arithmetic and copies ran while one was open for 18% of the time, Pallas kernels for 0%

profile of v1, /device:TPU:0, one launch (start us, length us, event | category | flops | bytes accessed | tf_op | source)
XLA Modules:
  0.0 1225.7 jit_solution(9680974198860835281)
XLA Ops:
  11.7 46.8 %all-gather.11.cloned.1.call-done = bf16[3,1024,512]{2,1,0:T(8,128)(2,1)} async-done(((bf16[3,64,512]{2,1,0:T(8,128)(2,1)}), bf16[3,1024,512]{2,1,0:T(8,128)(2,1)}) %all-gather.11.cloned.1.call-update) | async-done | bytes 3145744 | tf_op jit(solution)/shard_map/all_gather | solution.py:79
  58.5 4.7 fusion.83
  68.2 13.2 %all-gather.2 = s32[4,1,640]{2,1,0:T(1,128)S(1)} all-gather(s32[1,1,640]{2,1,0:T(1,128)S(1)} %reshape.676), channel_id=1, replica_groups=mesh['shard'=4,'ctx'=4,'tp'=2] {'ctx'}, dimensions={0}, use_global_device_ids=true | all-gather | bytes 12800 | tf_op jit(solution)/shard_map/all_gather | solution.py:83
  81.5 13.3 %all-gather.3 = s32[4,1,640]{2,1,0:T(1,128)S(1)} all-gather(s32[1,1,640]{2,1,0:T(1,128)S(1)} %reshape.678), channel_id=1, replica_groups=mesh['shard'=4,'ctx'=4,'tp'=2] {'ctx'}, dimensions={0}, use_global_device_ids=true | all-gather | bytes 12800 | tf_op jit(solution)/shard_map/all_gather | solution.py:84
  94.9 32.4 %select_select_fusion = (s32[640]{0:T(1024)S(1)}, s32[640]{0:T(1024)S(1)}) fusion(s32[]{:T(128)} %bitcast.57, s32[]{:T(128)} %bitcast.56, s32[]{:T(128)} %bitcast.55, s32[]{:T(128)} %bitcast.54, s32[]{:T(128)} %bitcast.53, s32[]{:T(128)} %bitcast.52, s32[]{:T(128)} %bitcast.51, s32[]{:T(128)} %bitcast.50, s32[]{:T(128)} %bitcast.49, s32[]{:T(128)} %bitcast.48, ...), kind=kLoop, calls=%fused_computation.139 | loop fusion | flops 139520 | bytes 7888 | tf_op jit(solution)/shard_map/jit(_take)/select_n | solution.py:30
  127.3 7.1 reshape.547
  139.0 34.5 %all-gather.21.cloned.1.call-done = bf16[1,2560,512]{1,2,0:T(8,128)(2,1)} async-done(((bf16[1,640,512]{1,2,0:T(8,128)(2,1)}), bf16[1,2560,512]{1,2,0:T(8,128)(2,1)}) %all-gather.21.cloned.1.call-update) | async-done | bytes 2621456 | tf_op jit(solution)/shard_map/all_gather | solution.py:96
  173.6 7.0 reshape.550
  180.6 4.7 copy.61
  185.3 41.6 %while.39 = (s32[]{:T(128)}, f32[8,640]{1,0:T(8,128)S(1)}, f32[8,640]{1,0:T(8,128)S(1)}, s32[5,512]{1,0:T(8,128)S(1)}, s32[640]{0:T(1024)S(1)}, /*index=5*/s32[6...) while((s32[]{:T(128)}, f32[8,640]{1,0:T(8,128)S(1)}, ...), condition=%wide.region_5.7_spmd.clone, body=%wide.region_2.6_spmd.clone.sunk | while | flops 367354912 | bytes 27360004 | solution.py:122
  185.9 4.8 select_reduce_fusion.2
  194.2 4.7 select_reduce_fusion.2
  202.5 4.8 select_reduce_fusion.2
  210.9 4.8 select_reduce_fusion.2
  219.2 4.8 select_reduce_fusion.2
  226.9 40.9 %while.40 = (s32[]{:T(128)}, f32[640,8,64]{0,2,1:T(8,128)}, bf16[5,512,8,64]{1,3,2,0:T(8,128)(2,1)}, s32[5,512]{1,0:T(8,128)S(1)}, s32[640]{0:T(1024)S(1)}, /*in...) while((s32[]{:T(128)}, f32[640,8,64]{0,2,1:T(8,128)}, ...), condition=%wide.region_7.9_spmd.clone, body=%wide.region_6.8_spmd.clone.sunk | while | flops 693043264 | bytes 7672046 | solution.py:136
  227.8 7.2 fusion.154
  235.6 7.6 fusion.154
  243.8 7.6 fusion.154
  252.0 7.6 fusion.154
  260.2 7.6 fusion.154
  274.1 43.2 %all-reduce.9.cloned.1.call-done = bf16[640,1024]{1,0:T(8,128)(2,1)} async-done(((bf16[640,1024]{1,0:T(8,128)(2,1)}), bf16[640,1024]{1,0:T(8,128)(2,1)}) %all-reduce.9.cloned.1.call-update) | async-done | bytes 1310736 | tf_op jit(solution)/shard_map/psum | solution.py:143
  319.9 50.4 %all-gather.15.cloned.1.call-done = bf16[1024,2048]{1,0:T(8,128)(2,1)} async-done(((bf16[64,2048]{1,0:T(8,128)(2,1)}), bf16[1024,2048]{1,0:T(8,128)(2,1)}) %all-gather.15.cloned.1.call-update) | async-done | bytes 4194320 | tf_op jit(solution)/shard_map/all_gather | solution.py:153
  370.3 7.7 fusion.95
  378.1 43.8 %all-gather.17.cloned.1.call-done = bf16[2048,1024]{0,1:T(8,128)(2,1)} async-done(((bf16[2048,64]{0,1:T(8,128)(2,1)}), bf16[2048,1024]{0,1:T(8,128)(2,1)}) %all-gather.17.cloned.1.call-update) | async-done | bytes 4194320 | tf_op jit(solution)/shard_map/all_gather | solution.py:154
  421.8 9.6 convert_reduce_fusion
  437.1 44.3 %all-reduce.11.cloned.1.call-done = bf16[640,1024]{1,0:T(8,128)(2,1)} async-done(((bf16[640,1024]{1,0:T(8,128)(2,1)}), bf16[640,1024]{1,0:T(8,128)(2,1)}) %all-reduce.11.cloned.1.call-update) | async-done | bytes 1310736 | tf_op jit(solution)/shard_map/psum | solution.py:178
  489.5 80.3 %while.41 = (s32[]{:T(128)}, f32[640,8,64]{0,2,1:T(8,128)S(1)}, bf16[5,512,512]{1,2,0:T(8,128)(2,1)}, bf16[5,512,512]{1,2,0:T(8,128)(2,1)}, bf16[5,512,8,64]{1,3...) while((s32[]{:T(128)}, f32[640,8,64]{0,2,1:T(8,128)S(1)}, ...), condition=%wide.region_16.18_spmd.clone, body=%wide.region_15.17_spmd.clone.sunk | while | flops 1708392448 | bytes 60513056 | solution.py:228
  490.1 5.1 fusion.165
  506.1 5.1 fusion.165
  522.2 5.1 fusion.165
  538.3 5.1 fusion.165
  554.3 5.1 fusion.165
  579.3 8.7 convolution_convert_fusion.1
  588.5 37.9 %reduce-scatter.8.cloned.1.call-done = bf16[640,512]{1,0:T(8,128)(2,1)} async-done(((bf16[2560,512]{1,0:T(8,128)(2,1)}), bf16[640,512]{1,0:T(8,128)(2,1)}) %reduce-scatter.8.cloned.1.call-update) | async-done | bytes 655376 | tf_op jit(solution)/shard_map/reduce_scatter | solution.py:240
  626.4 54.0 %reduce-scatter.6.cloned.1.call-done = bf16[640,512]{1,0:T(8,128)(2,1)} async-done(((bf16[2560,512]{1,0:T(8,128)(2,1)}), bf16[640,512]{1,0:T(8,128)(2,1)}) %reduce-scatter.6.cloned.1.call-update) | async-done | bytes 655376 | tf_op jit(solution)/shard_map/reduce_scatter | solution.py:234
  680.4 5.6 bitcast_convert_fusion
  687.5 5.8 convolution_bitcast_fusion
  693.3 9.4 copy.68
  708.0 9.7 fusion.96
  719.0 7.7 fusion.94
  728.9 31.6 %all-reduce.15.cloned.1.call-done = (bf16[640,1024]{1,0:T(8,128)(2,1)}, bf16[640,1024]{1,0:T(8,128)(2,1)}) async-done(((bf16[640,1024]{1,0:T(8,128)(2,1)}, bf16[640,1024]{1,0:T(8,128)(2,1)}), (bf16[640,1024]{1,0:T(8,128)(2,1)}, bf16[640,1024]{1,0:T(8,128)(2,1)})) %all-reduce.15.cloned.1.call-update) | async-done | bytes 2621456 | tf_op jit(solution)/shard_map/psum | solution.py:162
  763.1 20.4 %all-reduce.1 = (f32[2,512]{1,0:T(2,128)S(1)}, f32[1024]{0:T(1024)S(1)}, f32[2048]{0:T(1024)S(1)}, f32[1024]{0:T(1024)S(1)}, f32[2,1024]{1,0:T(2,128)S(1)}, /*index=5*/f32[2,1024]{1,0:T(2,128)S(1)}) all-reduce(f32[2,512]{1,0:T(2,128)S(1)} %pad_maximum_fusion.6, ...), channel_id=1, replica_groups=mesh['shard'=4,'ctx'=4,'tp'=2] {'ctx'}, use_global_device_ids=true, to_apply=%region_25.27 | all-reduce | flops 9216 | bytes 73728 | tf_op jit(solution)/shard_map/psum | solution.py:277
  783.4 12.0 all-reduce.2
  800.0 135.1 %all-reduce.13.cloned.1.call-done = f32[3,1024,512]{2,0,1:T(4,128)} async-done(((f32[3,1024,512]{2,0,1:T(4,128)}), f32[3,1024,512]{2,0,1:T(4,128)}) %all-reduce.13.cloned.1.call-update) | async-done | bytes 6291472
  937.1 63.7 %reduce-scatter.10.cloned.1.call-done = f32[512,64]{0,1:T(8,128)} async-done(((f32[512,1024]{0,1:T(8,128)}), f32[512,64]{0,1:T(8,128)}) %reduce-scatter.10.cloned.1.call-update) | async-done | bytes 131088 | tf_op jit(solution)/shard_map/reduce_scatter | solution.py:261
  1000.9 108.6 %reduce-scatter.14.cloned.1.call-done = f32[2048,64]{0,1:T(8,128)} async-done(((f32[2048,1024]{0,1:T(8,128)}), f32[2048,64]{0,1:T(8,128)}) %reduce-scatter.14.cloned.1.call-update) | async-done | bytes 524304 | tf_op jit(solution)/shard_map/reduce_scatter | solution.py:176
  1109.5 109.4 %reduce-scatter.12.cloned.1.call-done = f32[64,2048]{1,0:T(8,128)} async-done(((f32[1024,2048]{1,0:T(8,128)}), f32[64,2048]{1,0:T(8,128)}) %reduce-scatter.12.cloned.1.call-update) | async-done | bytes 524304 | tf_op jit(solution)/shard_map/reduce_scatter | solution.py:175
  (298 shorter events, 139.8 us)
Async XLA Ops:
  7.2 51.3 %copy-start = (bf16[640,1024]{1,0:T(8,128)(2,1)S(1)}, bf16[640,1024]{1,0:T(8,128)(2,1)}, u32[]{:S(2)}) copy-start(bf16[640,1024]{1,0:T(8,128)(2,1)} %param.23) | copy-start | bytes 3932164
  7.2 4.3 copy-start.40
  7.2 4.4 copy-start.36
  7.2 4.4 copy-start.37
  7.2 51.2 %all-gather.11.cloned.1.call-start = ((), (), s32[]{:S(2)}) async-start(), calls=%async_computation.5 | async-start | bytes 3342336 | tf_op jit(solution)/shard_map/all_gather | solution.py:79
  8.0 119.3 %all-gather.19.cloned.1.call-start = ((), (), s32[]{:S(2)}) async-start(), calls=%async_computation.16 | async-start | bytes 3276800 | tf_op jit(solution)/shard_map/all_gather | solution.py:97
  9.6 48.8 %copy-start.20 = (f32[640]{0:T(1024)}, f32[640]{0:T(1024)S(1)}, u32[]{:S(2)}) copy-start(f32[640]{0:T(1024)S(1)} %broadcast_multiply_fusion.5) | copy-start | bytes 7684
  11.5 51.7 %copy-start.24 = (f32[640]{0:T(1024)}, f32[640]{0:T(1024)S(1)}, u32[]{:S(2)}) copy-start(f32[640]{0:T(1024)S(1)} %add_rsqrt_fusion.1) | copy-start | bytes 7684
  11.6 51.6 %copy-start.26 = (f32[1,1024]{1,0:T(1,128)}, f32[1,1024]{1,0:T(1,128)S(1)}, u32[]{:S(2)}) copy-start(f32[1,1024]{1,0:T(1,128)S(1)} %get-tuple-element.698) | copy-start | bytes 12292
  11.6 473.8 %copy-start.30 = (f32[1,1024]{1,0:T(1,128)}, f32[1,1024]{1,0:T(1,128)S(1)}, u32[]{:S(2)}) copy-start(f32[1,1024]{1,0:T(1,128)S(1)} %get-tuple-element.699) | copy-start | bytes 12292
  11.6 51.6 %copy-start.43 = (f32[1,1024]{1,0:T(1,128)}, f32[1,1024]{1,0:T(1,128)S(1)}, u32[]{:S(2)}) copy-start(f32[1,1024]{1,0:T(1,128)S(1)} %get-tuple-element.700) | copy-start | bytes 12292
  11.6 358.7 %copy-start.41 = (f32[1,1024]{1,0:T(1,128)}, f32[1,1024]{1,0:T(1,128)S(1)}, u32[]{:S(2)}) copy-start(f32[1,1024]{1,0:T(1,128)S(1)} %get-tuple-element.701) | copy-start | bytes 12292
  63.2 2.8 copy-start.11
  63.2 4.9 copy-start.8
  63.3 4.9 copy-start.14
  64.6 108.9 %all-gather.21.cloned.1.call-start = ((), (), s32[]{:S(2)}) async-start(), calls=%async_computation.17 | async-start | bytes 3276800 | tf_op jit(solution)/shard_map/all_gather | solution.py:96
  65.4 203.9 %all-gather.13.cloned.1.call-start = ((), (), s32[]{:S(2)}) async-start(), calls=%async_computation.6 | async-start | bytes 1114112 | tf_op jit(solution)/shard_map/all_gather | solution.py:80
  65.9 251.3 %all-reduce.9.cloned.1.call-start = ((), (), s32[]{:S(2)}) async-start(), calls=%async_computation.7 | async-start | bytes 2621440 | tf_op jit(solution)/shard_map/psum | solution.py:143
  269.2 4.1 copy-start.9
  269.3 48.0 %copy-start.18 = (f32[1024]{0:T(1024)S(1)}, f32[1024]{0:T(1024)}, u32[]{:S(2)}) copy-start(f32[1024]{0:T(1024)} %param.31) | copy-start | bytes 12292
  272.7 97.6 %all-gather.15.cloned.1.call-start = ((), (), s32[]{:S(2)}) async-start(), calls=%async_computation.8 | async-start | bytes 4456448 | tf_op jit(solution)/shard_map/all_gather | solution.py:153
  273.3 148.5 %all-gather.17.cloned.1.call-start = ((), (), s32[]{:S(2)}) async-start(), calls=%async_computation.9 | async-start | bytes 4456448 | tf_op jit(solution)/shard_map/all_gather | solution.py:154
  274.1 207.4 %all-reduce.11.cloned.1.call-start = ((), (), s32[]{:S(2)}) async-start(), calls=%async_computation.10 | async-start | bytes 2621440 | tf_op jit(solution)/shard_map/psum | solution.py:178
  319.2 166.2 %copy-start.22 = (f32[640]{0:T(1024)}, f32[640]{0:T(1024)S(1)}, u32[]{:S(2)}) copy-start(f32[640]{0:T(1024)S(1)} %broadcast_multiply_fusion.4) | copy-start | bytes 7684
  319.9 165.5 %copy-start.28 = (f32[640]{0:T(1024)}, f32[640]{0:T(1024)S(1)}, u32[]{:S(2)}) copy-start(f32[640]{0:T(1024)S(1)} %add_rsqrt_fusion) | copy-start | bytes 7684
  370.3 51.5 %copy-start.47 = (f32[2048]{0:T(1024)S(1)}, f32[2048]{0:T(1024)}, u32[]{:S(2)}) copy-start(f32[2048]{0:T(1024)} %param.33) | copy-start | bytes 24580
  421.8 11.1 copy-start.45
  437.0 189.4 %reduce-scatter.8.cloned.1.call-start = ((), (), s32[]{:S(2)}) async-start(), calls=%async_computation.12 | async-start | bytes 3276800 | tf_op jit(solution)/shard_map/reduce_scatter | solution.py:240
  481.4 4.0 copy-start.4
  481.4 4.0 copy-start.7
  481.4 4.0 copy-start.12
  485.4 2.6 copy-start.6
  485.4 2.5 copy-start.15
  574.1 106.2 %reduce-scatter.6.cloned.1.call-start = ((), (), s32[]{:S(2)}) async-start(), calls=%async_computation.11 | async-start | bytes 3276800 | tf_op jit(solution)/shard_map/reduce_scatter | solution.py:234
  578.6 181.8 %all-reduce.15.cloned.1.call-start = ((), (), s32[]{:S(2)}) async-start(), calls=%async_computation.19 | async-start | bytes 5242880 | tf_op jit(solution)/shard_map/psum | solution.py:162
  680.4 5.8 copy-start.46
  686.1 249.0 %all-reduce.13.cloned.1.call-start = ((), (), s32[]{:S(2)}) async-start(), calls=%async_computation.18 | async-start | bytes 16777216
  702.8 5.2 copy-start.13
  702.8 298.1 %reduce-scatter.10.cloned.1.call-start = ((), (), s32[]{:S(2)}) async-start(), calls=%async_computation.13 | async-start | bytes 2228224 | tf_op jit(solution)/shard_map/reduce_scatter | solution.py:261
  707.9 401.6 %reduce-scatter.14.cloned.1.call-start = ((), (), s32[]{:S(2)}) async-start(), calls=%async_computation.15 | async-start | bytes 8912896 | tf_op jit(solution)/shard_map/reduce_scatter | solution.py:176
  717.7 501.2 %reduce-scatter.12.cloned.1.call-start = ((), (), s32[]{:S(2)}) async-start(), calls=%async_computation.14 | async-start | bytes 8912896 | tf_op jit(solution)/shard_map/reduce_scatter | solution.py:175
  726.8 2.0 copy-start.17
  726.8 36.2 %copy-start.35 = (f32[1024]{0:T(1024)S(1)}, f32[1024]{0:T(1024)}, u32[]{:S(2)}) copy-start(f32[1024]{0:T(1024)} %get-tuple-element.566) | copy-start | bytes 12292
  726.8 36.2 %copy-start.34 = (f32[1024]{0:T(1024)S(1)}, f32[1024]{0:T(1024)}, u32[]{:S(2)}) copy-start(f32[1024]{0:T(1024)} %get-tuple-element.573) | copy-start | bytes 12292
  726.8 36.2 %copy-start.32 = (f32[1024]{0:T(1024)S(1)}, f32[1024]{0:T(1024)}, u32[]{:S(2)}) copy-start(f32[1024]{0:T(1024)} %get-tuple-element.678) | copy-start | bytes 12292
  726.8 36.2 %copy-start.33 = (f32[1024]{0:T(1024)S(1)}, f32[1024]{0:T(1024)}, u32[]{:S(2)}) copy-start(f32[1024]{0:T(1024)} %get-tuple-element.695) | copy-start | bytes 12292
  726.8 36.2 %copy-start.38 = (f32[2048]{0:T(1024)S(1)}, f32[2048]{0:T(1024)}, u32[]{:S(2)}) copy-start(f32[2048]{0:T(1024)} %get-tuple-element.676) | copy-start | bytes 24580
  726.9 68.6 %copy-start.39 = (f32[1024]{0:T(1024)S(1)}, f32[1024]{0:T(1024)}, u32[]{:S(2)}) copy-start(f32[1024]{0:T(1024)} %param.35) | copy-start | bytes 12292
  (18 other events, 24.0 us)
Sparse Core Ops, SparseCore 0:
  10.3 48.1 all-gather.10
  64.7 53.8 all-gather.18
  120.2 53.3 all-gather.20
  175.6 36.6 all-gather.12
  272.8 44.3 all-reduce.8
  319.6 50.6 all-gather.14
  372.8 49.0 all-gather.16
  437.1 44.2 all-reduce.10
  574.2 52.0 reduce-scatter.7
  628.5 51.7 reduce-scatter.5
  686.2 74.2 all-reduce.14
  764.5 170.5 all-reduce.12
  939.4 61.3 reduce-scatter.9
  1005.9 103.5 reduce-scatter.13
  1114.5 104.3 reduce-scatter.11
